TPU v7x, 128 devices: a whole 4x4x4 slice. The times are simulated.
128 devices in a mesh: slab: 8 (over y, x_hi), brick: 16 (over x_lo, z, core).
Axes of the slice: x: 4 (x_hi: 2, x_lo: 2; x = x_hi * 2 + x_lo), y: 4, z: 4, core: 2. Of those that a mesh axis runs over, the one named last changes fastest.
Arguments:
- k_coeffs: float32 [16, 32, 16, 128], P('slab', 'brick'), may hold values from -0.3 to 0.4
- v_basis: float32 [32768, 128], P(('slab', 'brick')), may hold values from -4 to 4
Outputs:
- basis_x: float32 [16, 32, 16, 128], P('slab', 'brick')
- coupling: float32 [128, 128], replicated
- basis_v: float32 [32768, 128], P(('slab', 'brick'))
All inputs are finite; a program needn't handle non-finite values.
Results may differ from a plain program's by a relative error of at most 0.0001.
Values sent between devices are 32-bit elements; how exact they have to be, the bound alone decides.
No kernel may reach another device: no remote copies, remote signals or barrier semaphores. Data moves between devices by JAX's collectives and lax.ppermute only.
A program may use at most 64 MiB of HBM per device.

v0:
```python
import math
import jax
import jax.numpy as jnp
from jax import lax
from jax.sharding import PartitionSpec as P

NVX = 32
CFL = 0.9
VMAX = 6.0
COLLIDE = 0.3
RHO_MIN = 0.25
TEMP_MIN = 0.25
PRECISE = lax.Precision.HIGHEST


def with_halo(array, sides, width):
    edges = {}
    for axis, dim in sides:
        peers, length = (lax.axis_size(axis), array.shape[dim])
        up = [(i, (i + 1) % peers) for i in range(peers)]
        last = lax.slice_in_dim(array, length - width, length, axis=dim)
        leading = lax.slice_in_dim(array, 0, width, axis=dim)
        edges[dim] = (
            lax.ppermute(last, axis, up),
            lax.ppermute(leading, axis, [(b, a) for a, b in up]),
        )
    done = []
    for _, dim in sides:
        low, high = edges[dim]
        around = [(width, width) if d in done else (0, 0) for d in range(array.ndim)]
        array = jnp.concatenate([jnp.pad(low, around), array, jnp.pad(high, around)], axis=dim)
        done.append(dim)
    return array


def over_pieces(array, axis):
    parts = lax.all_gather(array, axis)
    return parts.sum(axis=0)


def velocities(indices):
    spacing = 2.0 * VMAX / NVX
    first_index = indices // (NVX * NVX)
    second = indices // NVX % NVX
    third_index = indices % NVX
    coords = jnp.stack([first_index, second, third_index]).astype(jnp.float32)
    return -VMAX + (coords + 0.5) * spacing


def maxwell(cell_params, velocity):
    distance = (velocity[0][None, :] - cell_params[1][:, None]) ** 2
    distance = distance + (velocity[1][None, :] - cell_params[2][:, None]) ** 2
    distance = distance + (velocity[2][None, :] - cell_params[3][:, None]) ** 2
    amplitude = cell_params[0] * (2.0 * math.pi * cell_params[4]) ** (-1.5)
    return amplitude[:, None] * jnp.exp(distance * (-0.5 / cell_params[4])[:, None])


def cell_state(vectors, coeffs):
    moments = lax.dot_general(vectors, coeffs, (((1,), (1,)), ((), ())), precision=PRECISE)
    density = jnp.maximum(moments[0], RHO_MIN)
    drift_speed = moments[1:4] / density[None, :]
    temper = jnp.maximum(
        (moments[4] / density - jnp.sum(drift_speed * drift_speed, axis=0)) / 3.0, TEMP_MIN
    )
    return jnp.concatenate([density[None], drift_speed, temper[None]], axis=0)


def transport_flux(backward, forward, transport):
    flux = jnp.zeros_like(backward[0])
    for axis_id in range(3):
        flux = flux + jnp.dot(backward[axis_id], transport[axis_id], precision=PRECISE)
        flux = flux + jnp.dot(forward[axis_id], transport[3 + axis_id], precision=PRECISE)
    return flux


def products(left_side, backward, forward, maxwell_proj):
    pieces = [
        lax.dot_general(left_side, item, (((0,), (0,)), ((), ())), precision=PRECISE)
        for item in backward + forward + [maxwell_proj]
    ]
    return jnp.stack(pieces)


def coupling_step(coupling_hat, minus_side, plus_side, projected, transport, time_step):
    drift_sum = jnp.zeros_like(coupling_hat)
    for axis_id in range(3):
        drift_sum = drift_sum + jnp.dot(
            jnp.dot(minus_side[axis_id], coupling_hat, precision=PRECISE),
            transport[axis_id],
            precision=PRECISE,
        )
        drift_sum = drift_sum + jnp.dot(
            jnp.dot(plus_side[axis_id], coupling_hat, precision=PRECISE),
            transport[3 + axis_id],
            precision=PRECISE,
        )
    return coupling_hat + time_step * drift_sum - COLLIDE * (projected - coupling_hat)


def velocity_step(velocity_part, minus_side, plus_side, back_proj, positive, negative, time_step):
    drift_sum = jnp.zeros_like(velocity_part)
    for axis_id in range(3):
        drift_sum = drift_sum + positive[axis_id][:, None] * jnp.dot(
            velocity_part, minus_side[axis_id].T, precision=PRECISE
        )
        drift_sum = drift_sum + negative[axis_id][:, None] * jnp.dot(
            velocity_part, plus_side[axis_id].T, precision=PRECISE
        )
    return velocity_part - time_step * drift_sum + COLLIDE * (back_proj - velocity_part)


def slopes(padded, lengths):
    rank_size = padded.shape[3]
    centre = padded[1:-1, 1:-1]
    backward = [
        (centre - padded[:-2, 1:-1]) * lengths[0],
        (centre - padded[1:-1, :-2]) * lengths[1],
        (centre - jnp.roll(centre, 1, axis=2)) * lengths[2],
    ]
    forward = [
        (padded[2:, 1:-1] - centre) * lengths[0],
        (padded[1:-1, 2:] - centre) * lengths[1],
        (jnp.roll(centre, -1, axis=2) - centre) * lengths[2],
    ]
    return (
        [item.reshape(-1, rank_size) for item in backward],
        [item.reshape(-1, rank_size) for item in forward],
    )


def local(k_coeffs, v_basis):
    cells_x, cells_y, cells_z, rank_size = k_coeffs.shape
    cell_count = cells_x * cells_y * cells_z
    slab_count = lax.axis_size("slab")
    brick_count = lax.axis_size("brick")
    devices = slab_count * brick_count
    lengths = (cells_x * slab_count, cells_y * brick_count, cells_z)
    time_step = CFL / (VMAX * (lengths[0] + lengths[1] + lengths[2]))
    weight_x = 1.0 / (lengths[0] * lengths[1] * lengths[2])
    weight_v = (2.0 * VMAX / NVX) ** 3
    row_count = v_basis.shape[0]
    device = lax.axis_index("slab") * brick_count + lax.axis_index("brick")
    row_ids = device * row_count + jnp.arange(row_count, dtype=jnp.int32)
    velocity = velocities(row_ids)
    positive = jnp.maximum(velocity, 0.0)
    negative = jnp.minimum(velocity, 0.0)
    weights = jnp.stack(
        [
            jnp.ones_like(velocity[0]),
            velocity[0],
            velocity[1],
            velocity[2],
            jnp.sum(velocity * velocity, axis=0),
        ]
    )
    vectors = jnp.dot(weights, v_basis, precision=PRECISE) * weight_v
    transport = jnp.stack(
        [
            lax.dot_general(
                v_basis * (side[axis_id] * weight_v)[:, None],
                v_basis,
                (((0,), (0,)), ((), ())),
                precision=PRECISE,
            )
            for side in (positive, negative)
            for axis_id in range(3)
        ]
    )
    transport, vectors = lax.psum((transport, vectors), ("slab", "brick"))
    coeff_flat = k_coeffs.reshape(cell_count, rank_size)
    cell_params = cell_state(vectors, coeff_flat)
    params_all = lax.all_gather(cell_params, ("slab", "brick"), axis=1, tiled=True)
    row_total = cell_count * devices
    block_rows = math.gcd(row_total, 512)

    def one_block(turn_index):
        part_params = lax.dynamic_slice_in_dim(
            params_all, 0 + turn_index * block_rows, block_rows, 1
        )
        return jnp.dot(maxwell(part_params, velocity), v_basis, precision=PRECISE) * weight_v

    blocks = lax.map(one_block, jnp.arange(row_total // block_rows, dtype=jnp.int32))
    whole_term = lax.psum(blocks.reshape(row_total, rank_size), ("slab", "brick"))
    maxwell_proj = lax.dynamic_slice_in_dim(whole_term, device * cell_count, cell_count, 0)
    padded = with_halo(k_coeffs, (("slab", 0), ("brick", 1)), 1)
    backward, forward = slopes(padded, lengths)
    advanced = (
        coeff_flat
        - time_step * transport_flux(backward, forward, transport)
        + COLLIDE * (maxwell_proj - coeff_flat)
    )
    identity = jnp.eye(rank_size, dtype=jnp.float32)
    padded_new = with_halo(
        advanced.reshape(cells_x, cells_y, cells_z, rank_size), (("slab", 0), ("brick", 1)), 1
    )
    backward, forward = slopes(padded_new, lengths)
    local_sums = jnp.concatenate(
        [
            lax.dot_general(advanced, advanced, (((0,), (0,)), ((), ())), precision=PRECISE)[None],
            products(advanced, backward, forward, maxwell_proj),
        ],
        axis=0,
    )
    reduced_all = lax.psum(local_sums * weight_x, ("slab", "brick"))
    factor = jnp.linalg.cholesky(reduced_all[0])
    inverse = jax.scipy.linalg.solve_triangular(factor, identity, lower=True)
    basis_new = jnp.dot(advanced, inverse.T, precision=PRECISE)
    mapped = jnp.einsum("ab,kbc,dc->kad", inverse, reduced_all[1:7], inverse, precision=PRECISE)
    minus_side = mapped[0:3]
    plus_side = mapped[3:6]
    projected = jnp.dot(inverse, reduced_all[7], precision=PRECISE)
    coupling_mid = coupling_step(factor.T, minus_side, plus_side, projected, transport, time_step)
    rows_piece = lax.all_gather(basis_new, ("slab", "brick"), axis=0, tiled=True)
    piece_rows = rows_piece.shape[0]
    fold_block_rows = math.gcd(piece_rows, 512)

    def add_block(turn_index, accumulated):
        offset = turn_index * fold_block_rows
        part_params = lax.dynamic_slice_in_dim(params_all, offset, fold_block_rows, 1)
        basis_block = lax.dynamic_slice_in_dim(rows_piece, offset, fold_block_rows, 0)
        values = maxwell(part_params, velocity)
        return (
            accumulated
            + lax.dot_general(values, basis_block, (((0,), (0,)), ((), ())), precision=PRECISE)
            * weight_x
        )

    back_proj = lax.fori_loop(
        0, piece_rows // fold_block_rows, add_block, jnp.zeros((row_count, rank_size), jnp.float32)
    )
    velocity_part = jnp.dot(v_basis, coupling_mid.T, precision=PRECISE)
    velocity_new = velocity_step(
        velocity_part, minus_side, plus_side, back_proj, positive, negative, time_step
    )
    gram_v = (
        lax.dot_general(velocity_new, velocity_new, (((0,), (0,)), ((), ())), precision=PRECISE)
        * weight_v
    )
    gram_v = over_pieces(gram_v, ("slab", "brick"))
    coupling = jnp.linalg.cholesky(gram_v)
    inverse_v = jax.scipy.linalg.solve_triangular(coupling, identity, lower=True)
    vbasis_new = jnp.dot(velocity_new, inverse_v.T, precision=PRECISE)
    return (basis_new.reshape(cells_x, cells_y, cells_z, rank_size), coupling, vbasis_new)


def solution(mesh):
    placed = (P("slab", "brick", None, None), P(("slab", "brick"), None))
    return jax.shard_map(
        local,
        mesh=mesh,
        in_specs=placed,
        out_specs=(P("slab", "brick", None, None), P(), P(("slab", "brick"), None)),
        check_vma=False,
    )
```

profile of v0, /device:TPU:1, one launch (start us, length us, event | category | flops | bytes accessed | tf_op | source)
XLA Modules:
  0.0 735.6 jit_solution(13024606328633485945)
XLA Ops:
  8.4 68.7 %psum.29 = f32[5,128]{1,0:T(8,128)S(1)} all-reduce(f32[5,128]{1,0:T(8,128)S(1)} %convolution_multiply_fusion.9), channel_id=1, replica_groups=mesh['slab'=8,'brick'=16] {'slab','brick'}, use_global_device_ids=true, to_apply=%region_2.3 | all-reduce | flops 640 | bytes 5120 | tf_op jit(solution)/shard_map/psum | solution.py:169
  78.1 34.4 %all-gather.1 = f32[128,64,5]{1,2,0:T(8,128)S(1)} all-gather(f32[1,64,5]{1,2,0:T(8,128)S(1)} %maximum_bitcast_fusion), channel_id=1, replica_groups=mesh['slab'=8,'brick'=16] {'slab','brick'}, dimensions={0}, use_global_device_ids=true | all-gather | bytes 165120 | tf_op jit(solution)/shard_map/all_gather | solution.py:172
  112.7 60.6 %while.24 = (s32[]{:T(128)}, f32[16,512,128]{2,1,0:T(8,128)}, s32[16]{0:T(128)S(1)}, f32[5,8192]{1,0:T(8,128)S(1)}, f32[3,256]{1,0:T(4,128)S(1)}, /*index=5*/f32...) while((s32[]{:T(128)}, f32[16,512,128]{2,1,0:T(8,128)}, ...), condition=%wide.region_5.6_spmd, body=%wide.region_4.5_spmd.sunk | while | flops 202704400 | bytes 433923 | solution.py:182
  114.1 2.5 fusion.232
  117.9 2.4 fusion.232
  121.7 2.4 fusion.232
  136.8 2.4 fusion.232
  144.3 2.4 fusion.232
  151.9 2.4 fusion.232
  155.7 2.4 fusion.232
  167.0 2.5 fusion.232
  170.8 2.4 fusion.232
  184.1 3.9 collective-permute-start.1
  191.7 143.5 %all-reduce.10.cloned.1.call-done = (f32[6,128,128]{2,1,0:T(8,128)}, f32[8192,128]{1,0:T(8,128)}) async-done(((f32[6,128,128]{2,1,0:T(8,128)}, f32[8192,128]{1,0:T(8,128)}), (f32[6,128,128]{2,1,0:T(8,128)}, f32[8192,128]{1,0:T(8,128)})) %all-reduce.10.cloned.1.call-update) | async-done | bytes 4587536 | tf_op jit(solution)/shard_map/psum | solution.py:169
  344.1 4.2 collective-permute-start.6
  355.3 144.6 %all-reduce.8.cloned.1.call-done = f32[8,128,128]{1,2,0:T(8,128)} async-done(((f32[8,128,128]{1,2,0:T(8,128)}), f32[8,128,128]{1,2,0:T(8,128)}) %all-reduce.8.cloned.1.call-update) | async-done | bytes 524304 | tf_op jit(solution)/shard_map/psum | solution.py:204
  501.6 11.7 %cholesky.44 = f32[128,128]{1,0:T(8,128)S(1)} custom-call(f32[128,128]{1,0:T(8,128)S(1)} %fusion.83), custom_call_target="Cholesky" | custom-call | tf_op jit(solution)/shard_map/jit(cholesky)/cholesky | solution.py:205
  514.7 9.8 %custom-call.7 = f32[1,128,128]{1,2,0:T(8,128)S(1)} custom-call(f32[1,128,128]{2,1,0:T(8,128)S(1)} %select_bitcast_fusion.1), custom_call_target="InvertDiagBlocksLowerTriangular" | custom-call | tf_op jit(solution)/shard_map/jit(_solve_triangular)/triangular_solve | solution.py:206
  539.1 52.7 %all-gather.5.cloned.1.call-done = f32[8192,128]{1,0:T(8,128)} async-done(((f32[64,128]{1,0:T(8,128)}), f32[8192,128]{1,0:T(8,128)}) %all-gather.5.cloned.1.call-update) | async-done | bytes 4194320 | tf_op jit(solution)/shard_map/all_gather | solution.py:213
  591.8 39.5 %while.25 = (s32[]{:T(128)}, f32[256,128]{1,0:T(8,128)S(1)}, f32[5,8192]{1,0:T(8,128)S(1)}, f32[3,256]{1,0:T(4,128)S(1)}, f32[8192,128]{1,0:T(8,128)}, /*index=5...) while((s32[]{:T(128)}, f32[256,128]{1,0:T(8,128)S(1)}, ...), condition=%wide.region_11.14_spmd.clone, body=%wide.region_10.13_spmd.clone.sunk | while | flops 202737168 | bytes 564477 | solution.py:228
  632.6 67.7 %all-gather.7.cloned.1.call-done = f32[16384,128]{1,0:T(8,128)} async-done(((f32[128,128]{1,0:T(8,128)}), f32[16384,128]{1,0:T(8,128)}) %all-gather.7.cloned.1.call-update) | async-done | bytes 8388624 | tf_op jit(solution)/shard_map/all_gather | solution.py:37
  700.3 3.8 reduce_sum.32
  704.3 11.7 %cholesky.55 = f32[128,128]{1,0:T(8,128)S(1)} custom-call(f32[128,128]{1,0:T(8,128)S(1)} %fusion.85), custom_call_target="Cholesky" | custom-call | tf_op jit(solution)/shard_map/jit(cholesky)/cholesky | solution.py:240
  717.9 9.8 %custom-call.8 = f32[1,128,128]{1,2,0:T(8,128)S(1)} custom-call(f32[1,128,128]{2,1,0:T(8,128)S(1)} %get-tuple-element.175), custom_call_target="InvertDiagBlocksLowerTriangular" | custom-call | tf_op jit(solution)/shard_map/jit(_solve_triangular)/triangular_solve | solution.py:241
  (232 shorter events, 121.4 us)
Async XLA Ops:
  7.2 328.0 %all-reduce.10.cloned.1.call-start = ((), (), s32[]{:S(2)}) async-start(), calls=%async_computation.3 | async-start | bytes 9175040 | tf_op jit(solution)/shard_map/psum | solution.py:169
  173.3 9.6 %copy-start.1 = (f32[2,2,16,128]{3,2,1,0:T(8,128)S(1)}, f32[2,2,16,128]{3,2,1,0:T(8,128)}, u32[]{:S(2)}) copy-start(f32[2,2,16,128]{3,2,1,0:T(8,128)} %param.9) | copy-start | bytes 98308
  182.0 0.8 copy-start.3
  182.8 317.0 %all-reduce.8.cloned.1.call-start = ((), (), s32[]{:S(2)}) async-start(), calls=%async_computation | async-start | bytes 1048576 | tf_op jit(solution)/shard_map/psum | solution.py:204
  182.9 6.3 collective-permute-start
  184.1 5.0 collective-permute-start.1
  188.0 1.4 collective-permute-start.2
  188.0 3.6 collective-permute-start.3
  335.1 198.1 %copy-start.2 = (f32[6,128,128]{2,1,0:T(8,128)S(1)}, f32[6,128,128]{2,1,0:T(8,128)}, u32[]{:S(2)}) copy-start(f32[6,128,128]{2,1,0:T(8,128)} %get-tuple-element.173) | copy-start | bytes 1179652
  341.5 7.2 collective-permute-start.4
  343.1 5.5 collective-permute-start.5
  344.1 5.0 collective-permute-start.6
  348.3 3.2 collective-permute-start.7
  351.5 185.9 %copy-start = (f32[256,128]{1,0:T(8,128)S(1)}, f32[256,128]{1,0:T(8,128)}, u32[]{:S(2)}) copy-start(f32[256,128]{1,0:T(8,128)} %get-tuple-element.425) | copy-start | bytes 393220
  355.2 236.6 %all-gather.5.cloned.1.call-start = ((), (), s32[]{:S(2)}) async-start(), calls=%async_computation.1 | async-start | bytes 4227072 | tf_op jit(solution)/shard_map/all_gather | solution.py:213
  525.7 174.7 %all-gather.7.cloned.1.call-start = ((), (), s32[]{:S(2)}) async-start(), calls=%async_computation.2 | async-start | bytes 8454144 | tf_op jit(solution)/shard_map/all_gather | solution.py:37
Sparse Core Ops, SparseCore 0:
  182.9 152.1 all-reduce.9
  355.3 144.4 all-reduce.7
  525.8 65.9 all-gather.4
  632.7 67.5 all-gather.6
where the time goes:
time: 738 us; the launch traced here: 736 us
  waiting for transfers between devices  414 us (56%)
  matrix products  113 us (15%)
  blocking collectives  103 us (14%)
  other arithmetic  55 us (7%)
  between operations  14.3 us (2%)
  starting transfers between devices  12.9 us (2%)
  local copies, waits for them, and re-layouts  11.6 us (2%)
  loops' own time  11.5 us (2%)
    psum x1, waiting for transfers between devices, local(): reduced_all = lax.psum(local_sums * weight_x, ('slab', 'brick'))  145 us
    psum x1, waiting for transfers between devices, local(): transport, vectors = lax.psum((transport, vectors), ('slab', 'brick'))  143 us
    psum x1, blocking collectives, local(): transport, vectors = lax.psum((transport, vectors), ('slab', 'brick'))  68.7 us
    all_gather x1, waiting for transfers between devices, over_pieces(): parts = lax.all_gather(array, axis)  67.7 us
    all_gather x1, waiting for transfers between devices, local(): lax.all_gather(basis_new, ('slab', 'brick'), axis=0, tiled=True)  52.7 us
    dot_general x16, matrix products, one_block(): jnp.dot(maxwell(part_params, velocity), v_basis, precision=PRECISE)  38.9 us
    dot_general x16, matrix products, add_block(): lax.dot_general(values, basis_block, (((0,), (0,)), ((), ())), precision=...  37.2 us
    all_gather x1, blocking collectives, local(): lax.all_gather(cell_params, ('slab', 'brick'), axis=1, tiled=True)  34.4 us
  transfers between devices with their start and end apart: 12, of which 9 were waited for; matrix products, arithmetic and copies ran while one was open for 2% of the time, Pallas kernels for 0%

commit v1 on v0

--- a/solution.py
+++ b/solution.py
@@ -166,7 +166,7 @@
             for axis_id in range(3)
         ]
     )
-    transport, vectors = lax.psum((transport, vectors), ("slab", "brick"))
+    transport, vectors = lax.psum(lax.psum((transport, vectors), "slab"), "brick")
     coeff_flat = k_coeffs.reshape(cell_count, rank_size)
     cell_params = cell_state(vectors, coeff_flat)
     params_all = lax.all_gather(cell_params, ("slab", "brick"), axis=1, tiled=True)

time: 738 us -> 788 us (1.068)
  waiting for transfers between devices: 414 us -> 491 us
  blocking collectives: 103 us -> 85.6 us
  matrix products: 113 us -> 98.5 us
    psum x1 -> x3, waiting for transfers between devices: 143 us -> 223 us  [the longest x1 155 us: local(): lax.psum(blocks.reshape(row_total, rank_size), ('slab', 'brick'))]
    psum x1 -> x2, blocking collectives: 68.7 us -> 51.3 us  [the longest x1 32.3 us: local(): lax.psum(lax.psum((transport, vectors), 'slab'), 'brick')]
    dot_general x16, matrix products: 38.9 us -> 24.4 us  [one_block(): jnp.dot(maxwell(part_params, velocity), v_basis, precision=PRECISE)]
  transfers between devices with their start and end apart: 12 -> 14, of which waited for: 9 -> 7; matrix products, arithmetic and copies ran while one was open for 2% -> 7% of each run, Pallas kernels for 0% -> 0%
where the time goes in v1:
time: 788 us; the launch traced here: 786 us
  waiting for transfers between devices  491 us (62%)
  matrix products  98.5 us (12%)
  blocking collectives  85.6 us (11%)
  other arithmetic  55 us (7%)
  starting transfers between devices  15.9 us (2%)
  between operations  14.7 us (2%)
  local copies, waits for them, and re-layouts  13.8 us (2%)
  loops' own time  11.5 us (1%)
    psum x1, waiting for transfers between devices, local(): lax.psum(blocks.reshape(row_total, rank_size), ('slab', 'brick'))  155 us
    psum x1, waiting for transfers between devices, local(): reduced_all = lax.psum(local_sums * weight_x, ('slab', 'brick'))  144 us
    psum x1, waiting for transfers between devices, local(): lax.psum(lax.psum((transport, vectors), 'slab'), 'brick')  68.2 us
    all_gather x1, waiting for transfers between devices, over_pieces(): parts = lax.all_gather(array, axis)  67.7 us
    all_gather x1, waiting for transfers between devices, local(): lax.all_gather(basis_new, ('slab', 'brick'), axis=0, tiled=True)  52.7 us
    dot_general x16, matrix products, add_block(): lax.dot_general(values, basis_block, (((0,), (0,)), ((), ())), precision=...  37.2 us
    all_gather x1, blocking collectives, local(): lax.all_gather(cell_params, ('slab', 'brick'), axis=1, tiled=True)  34.3 us
    psum x1, blocking collectives, local(): lax.psum(lax.psum((transport, vectors), 'slab'), 'brick')  32.3 us
  transfers between devices with their start and end apart: 14, of which 7 were waited for; matrix products, arithmetic and copies ran while one was open for 7% of the time, Pallas kernels for 0%

profile of v1, /device:TPU:1, one launch (start us, length us, event | category | flops | bytes accessed | tf_op | source)
XLA Modules:
  0.0 785.8 jit_solution(14760448923321212404)
XLA Ops:
  17.6 3.6 collective-permute-start
  21.2 2.5 collective-permute-start.1
  24.4 2.6 collective-permute-start.2
  28.1 19.0 %psum.44 = f32[5,128]{1,0:T(8,128)S(1)} all-reduce(f32[5,128]{1,0:T(8,128)S(1)} %convolution_multiply_fusion.9), channel_id=1, replica_groups=mesh['slab'=8,'brick'=16] {'slab'}, use_global_device_ids=true, to_apply=%region_3.4 | all-reduce | flops 640 | bytes 5120 | tf_op jit(solution)/shard_map/psum | solution.py:169
  47.1 32.3 %psum.45 = f32[5,128]{1,0:T(8,128)S(1)} all-reduce(f32[5,128]{1,0:T(8,128)S(1)} %psum.44), channel_id=1, replica_groups=mesh['slab'=8,'brick'=16] {'brick'}, use_global_device_ids=true, to_apply=%region_4.5 | all-reduce | flops 640 | bytes 5120 | tf_op jit(solution)/shard_map/psum | solution.py:169
  80.4 34.3 %all-gather.1 = f32[128,64,5]{1,2,0:T(8,128)S(1)} all-gather(f32[1,64,5]{1,2,0:T(8,128)S(1)} %maximum_bitcast_fusion), channel_id=1, replica_groups=mesh['slab'=8,'brick'=16] {'slab','brick'}, dimensions={0}, use_global_device_ids=true | all-gather | bytes 165120 | tf_op jit(solution)/shard_map/all_gather | solution.py:172
  115.0 46.0 %while.24 = (s32[]{:T(128)}, f32[16,512,128]{2,1,0:T(8,128)}, s32[16]{0:T(128)S(1)}, f32[5,8192]{1,0:T(8,128)S(1)}, f32[3,256]{1,0:T(4,128)S(1)}, /*index=5*/f32...) while((s32[]{:T(128)}, f32[16,512,128]{2,1,0:T(8,128)}, ...), condition=%wide.region_7.8_spmd, body=%wide.region_6.7_spmd.sunk | while | flops 202704400 | bytes 433923 | solution.py:182
  162.0 68.2 %all-reduce.11.cloned.1.call-done = f32[6,128,128]{2,1,0:T(8,128)} async-done(((f32[6,128,128]{2,1,0:T(8,128)}), f32[6,128,128]{2,1,0:T(8,128)}) %all-reduce.11.cloned.1.call-update) | async-done | bytes 393232 | tf_op jit(solution)/shard_map/psum | solution.py:169
  235.4 154.9 %all-reduce.13.cloned.1.call-done = f32[8192,128]{1,0:T(8,128)} async-done(((f32[8192,128]{1,0:T(8,128)}), f32[8192,128]{1,0:T(8,128)}) %all-reduce.13.cloned.1.call-update) | async-done | bytes 4194320 | tf_op jit(solution)/shard_map/psum | solution.py:183
  394.0 4.2 collective-permute-start.6
  405.3 144.4 %all-reduce.15.cloned.1.call-done = f32[8,128,128]{1,2,0:T(8,128)} async-done(((f32[8,128,128]{1,2,0:T(8,128)}), f32[8,128,128]{1,2,0:T(8,128)}) %all-reduce.15.cloned.1.call-update) | async-done | bytes 524304 | tf_op jit(solution)/shard_map/psum | solution.py:204
  551.5 11.7 %cholesky.44 = f32[128,128]{1,0:T(8,128)S(1)} custom-call(f32[128,128]{1,0:T(8,128)S(1)} %fusion.83), custom_call_target="Cholesky" | custom-call | tf_op jit(solution)/shard_map/jit(cholesky)/cholesky | solution.py:205
  564.5 9.8 %custom-call.7 = f32[1,128,128]{1,2,0:T(8,128)S(1)} custom-call(f32[1,128,128]{2,1,0:T(8,128)S(1)} %select_bitcast_fusion.1), custom_call_target="InvertDiagBlocksLowerTriangular" | custom-call | tf_op jit(solution)/shard_map/jit(_solve_triangular)/triangular_solve | solution.py:206
  589.0 52.7 %all-gather.5.cloned.1.call-done = f32[8192,128]{1,0:T(8,128)} async-done(((f32[64,128]{1,0:T(8,128)}), f32[8192,128]{1,0:T(8,128)}) %all-gather.5.cloned.1.call-update) | async-done | bytes 4194320 | tf_op jit(solution)/shard_map/all_gather | solution.py:213
  641.6 39.5 %while.25 = (s32[]{:T(128)}, f32[256,128]{1,0:T(8,128)S(1)}, f32[5,8192]{1,0:T(8,128)S(1)}, f32[3,256]{1,0:T(4,128)S(1)}, f32[8192,128]{1,0:T(8,128)}, /*index=5...) while((s32[]{:T(128)}, f32[256,128]{1,0:T(8,128)S(1)}, ...), condition=%wide.region_13.16_spmd.clone, body=%wide.region_12.15_spmd.clone.sunk | while | flops 202737168 | bytes 564477 | solution.py:228
  644.2 2.3 fusion.236
  646.7 2.3 fusion.236
  649.1 2.3 fusion.236
  651.6 2.3 fusion.236
  654.1 2.3 fusion.236
  682.4 67.7 %all-gather.7.cloned.1.call-done = f32[16384,128]{1,0:T(8,128)} async-done(((f32[128,128]{1,0:T(8,128)}), f32[16384,128]{1,0:T(8,128)}) %all-gather.7.cloned.1.call-update) | async-done | bytes 8388624 | tf_op jit(solution)/shard_map/all_gather | solution.py:37
  750.2 3.8 reduce_sum.32
  754.1 11.7 %cholesky.55 = f32[128,128]{1,0:T(8,128)S(1)} custom-call(f32[128,128]{1,0:T(8,128)S(1)} %fusion.85), custom_call_target="Cholesky" | custom-call | tf_op jit(solution)/shard_map/jit(cholesky)/cholesky | solution.py:240
  767.8 9.8 %custom-call.8 = f32[1,128,128]{1,2,0:T(8,128)S(1)} custom-call(f32[1,128,128]{2,1,0:T(8,128)S(1)} %get-tuple-element.173), custom_call_target="InvertDiagBlocksLowerTriangular" | custom-call | tf_op jit(solution)/shard_map/jit(_solve_triangular)/triangular_solve | solution.py:241
  (239 shorter events, 114.7 us)
Async XLA Ops:
  7.2 107.9 %copy-start = (f32[256,128]{1,0:T(8,128)S(1)}, f32[256,128]{1,0:T(8,128)}, u32[]{:S(2)}) copy-start(f32[256,128]{1,0:T(8,128)} %param.10) | copy-start | bytes 393220
  7.2 107.8 %all-reduce.9.cloned.1.call-start = ((), (), s32[]{:S(2)}) async-start(), calls=%async_computation | async-start | bytes 786432 | tf_op jit(solution)/shard_map/psum | solution.py:169
  16.0 0.8 copy-start.3
  16.8 213.4 %all-reduce.11.cloned.1.call-start = ((), (), s32[]{:S(2)}) async-start(), calls=%async_computation.1 | async-start | bytes 786432 | tf_op jit(solution)/shard_map/psum | solution.py:169
  17.6 144.2 %collective-permute-start = (f32[1,2,16,128]{3,2,1,0:T(8,128)S(1)}, f32[1,2,16,128]{3,2,1,0:T(8,128)S(1)}, u32[]{:S(2)}, u32[]{:S(2)}) collective-permute-start(f32[1,2,16,128]{3,2,1,0:T(8,128)S(1)} %get-tuple-element.220), channel_id=1, source_target_pairs={{0,16},{16,32},{32,48},{48,64},{64,80},{80,96},{96,112},{112,0},{1... | collective-permute-start | bytes 49160 | tf_op jit(solution)/shard_map/ppermute | solution.py:24
  21.2 140.7 %collective-permute-start.1 = (f32[1,2,16,128]{3,2,1,0:T(8,128)S(1)}, f32[1,2,16,128]{3,2,1,0:T(8,128)S(1)}, u32[]{:S(2)}, u32[]{:S(2)}) collective-permute-start(f32[1,2,16,128]{3,2,1,0:T(8,128)S(1)} %get-tuple-element.219), channel_id=1, source_target_pairs={{16,0},{32,16},{48,32},{64,48},{80,64},{96,80},{112,96},{0,112},{1... | collective-permute-start | bytes 49160 | tf_op jit(solution)/shard_map/ppermute | solution.py:25
  24.4 137.5 %collective-permute-start.2 = (f32[2,1,16,128]{3,2,1,0:T(8,128)S(1)}, f32[2,1,16,128]{3,2,1,0:T(8,128)S(1)}, u32[]{:S(2)}, u32[]{:S(2)}) collective-permute-start(f32[2,1,16,128]{3,2,1,0:T(8,128)S(1)} %get-tuple-element.218), channel_id=1, source_target_pairs={{0,1},{1,2},{2,3},{3,4},{4,5},{5,6},{6,7},{7,8},{8,9},{9,10},{10,1... | collective-permute-start | bytes 49160 | tf_op jit(solution)/shard_map/ppermute | solution.py:24
  27.0 134.9 %collective-permute-start.3 = (f32[2,1,16,128]{3,2,1,0:T(8,128)S(1)}, f32[2,1,16,128]{3,2,1,0:T(8,128)S(1)}, u32[]{:S(2)}, u32[]{:S(2)}) collective-permute-start(f32[2,1,16,128]{3,2,1,0:T(8,128)S(1)} %get-tuple-element.217), channel_id=1, source_target_pairs={{1,0},{2,1},{3,2},{4,3},{5,4},{6,5},{7,6},{8,7},{9,8},{10,9},{11,1... | collective-permute-start | bytes 49160 | tf_op jit(solution)/shard_map/ppermute | solution.py:25
  115.0 275.3 %all-reduce.13.cloned.1.call-start = ((), (), s32[]{:S(2)}) async-start(), calls=%async_computation.2 | async-start | bytes 8388608 | tf_op jit(solution)/shard_map/psum | solution.py:183
  161.1 0.8 copy-start.1
  161.1 388.6 %all-reduce.15.cloned.1.call-start = ((), (), s32[]{:S(2)}) async-start(), calls=%async_computation.3 | async-start | bytes 1048576 | tf_op jit(solution)/shard_map/psum | solution.py:204
  230.2 352.9 %copy-start.2 = (f32[6,128,128]{2,1,0:T(8,128)S(1)}, f32[6,128,128]{2,1,0:T(8,128)}, u32[]{:S(2)}) copy-start(f32[6,128,128]{2,1,0:T(8,128)} %all-reduce.11.cloned.1.call-done) | copy-start | bytes 1179652
  391.4 7.1 collective-permute-start.4
  393.0 5.5 collective-permute-start.5
  394.0 5.1 collective-permute-start.6
  398.2 3.2 collective-permute-start.7
  405.1 236.6 %all-gather.5.cloned.1.call-start = ((), (), s32[]{:S(2)}) async-start(), calls=%async_computation.4 | async-start | bytes 4227072 | tf_op jit(solution)/shard_map/all_gather | solution.py:213
  575.5 174.7 %all-gather.7.cloned.1.call-start = ((), (), s32[]{:S(2)}) async-start(), calls=%async_computation.5 | async-start | bytes 8454144 | tf_op jit(solution)/shard_map/all_gather | solution.py:37
Sparse Core Ops, SparseCore 0:
  16.9 83.0 all-reduce.8
  115.1 115.0 all-reduce.10
  235.1 155.1 all-reduce.12
  405.2 144.4 all-reduce.14
  575.6 65.9 all-gather.4
  682.6 67.5 all-gather.6
